TPU v7x, 32 devices: a whole 2x2x4 slice. The times are simulated.
32 devices in a mesh: groups: 2 (over y), pts: 16 (over z, x, core).
Axes of the slice: x: 2, y: 2, z: 4, core: 2. Of those that a mesh axis runs over, the one named last changes fastest.
Arguments:
- latents: bfloat16 [2048, 768], P(('groups', 'pts')), parts along dimension 0, may hold values from -160 to 160
- points: bfloat16 [12288, 768], P(('groups', 'pts')), parts along dimension 0, may hold values from -6 to 6
- counts: int32 [32], P(('groups', 'pts')), parts along dimension 0, may hold values from 48 to 384, as said below
- w_query: bfloat16 [768, 768], replicated, may hold values from -0.21875 to 0.21875
- w_key: bfloat16 [768, 768], replicated, may hold values from -0.21875 to 0.21875
- w_value: bfloat16 [768, 768], replicated, may hold values from -0.21875 to 0.21875
- w_out: bfloat16 [768, 768], replicated, may hold values from -0.21875 to 0.21875
- d_out: bfloat16 [2048, 768], P(('groups', 'pts')), parts along dimension 0, may hold values from -6 to 6
Outputs:
- result: bfloat16 [2048, 768], P(('groups', 'pts')), parts along dimension 0
- d_latents: bfloat16 [2048, 768], P(('groups', 'pts')), parts along dimension 0
- d_points: bfloat16 [12288, 768], P(('groups', 'pts')), parts along dimension 0
There are 2 independent parts, one for each index of `groups`. A program takes and returns all parts, laid end to end along the dimension named above; an argument that names none is the same for every part. Nothing has to cross between parts.
Inputs may be any that keep to these rules, and one draw needn't show every extreme that they name: counts[s] live points fill the first slots of block s; in every part one block is full with 384 and another holds only 48.
All inputs are finite; a program needn't handle non-finite values.
Results may differ from a plain program's by a relative error of at most 0.018.
The roundings to bfloat16 on the way count: a program that leaves them out, or rounds other values in their place, can miss the bound.
Values may be sent and summed in bfloat16 or wider, within the bound.
No kernel may reach another device: no remote copies, remote signals or barrier semaphores. Data moves between devices by JAX's collectives and lax.ppermute only.
A program may use at most 128 MiB of HBM per device.

v0:
```python
import jax
import jax.numpy as jnp
from jax import lax
from jax.sharding import PartitionSpec as P

HEADS = 12


def masked_scores(query_head, key_head, live_mask):
    raw = jnp.dot(query_head, key_head.T, preferred_element_type=jnp.float32) * 0.125
    return jnp.where(live_mask[None, :], raw, -jnp.inf)


def body(latents, points, counts, w_query, w_key, w_value, w_out, d_out):
    own_rows, width = latents.shape
    slots = points.shape[0]
    head_dim = width // HEADS
    key_rows = jnp.dot(points, w_key, preferred_element_type=jnp.float32).astype(jnp.bfloat16)
    value_rows = jnp.dot(points, w_value, preferred_element_type=jnp.float32).astype(jnp.bfloat16)
    live_mask = jnp.arange(slots, dtype=jnp.int32) < counts[0]
    query_own = jnp.dot(latents, w_query, preferred_element_type=jnp.float32).astype(jnp.bfloat16)
    query_all = lax.all_gather(query_own, "pts", axis=0, tiled=True)
    query_count = query_all.shape[0]

    def split_heads(matrix):
        return matrix.reshape(matrix.shape[0], HEADS, head_dim).transpose(1, 0, 2)

    def join_heads(stack):
        return stack.transpose(1, 0, 2).reshape(stack.shape[1], width)

    query_heads = split_heads(query_all)
    key_heads = split_heads(key_rows)
    value_heads = split_heads(value_rows)

    def local_max(operands):
        query_head, key_head = operands
        return jnp.max(masked_scores(query_head, key_head, live_mask), axis=1)

    row_max = lax.pmax(lax.map(local_max, (query_heads, key_heads)), "pts")

    def partial_attend(operands):
        query_head, key_head, value_head, max_head = operands
        weights = jnp.exp(masked_scores(query_head, key_head, live_mask) - max_head[:, None])
        numerator = jnp.dot(
            weights.astype(jnp.bfloat16), value_head, preferred_element_type=jnp.float32
        )
        return (jnp.sum(weights, axis=1), numerator)

    totals, numerators = lax.map(partial_attend, (query_heads, key_heads, value_heads, row_max))
    numerator = join_heads(numerators)
    total_cols = totals.T
    start = lax.axis_index("pts") * own_rows
    grad_attended = jnp.dot(d_out, w_out.T, preferred_element_type=jnp.float32).astype(jnp.bfloat16)
    numer_all, total_all = lax.psum((numerator, total_cols), "pts")
    attended_all = (numer_all / jnp.repeat(total_all, head_dim, axis=1)).astype(jnp.bfloat16)
    attended = lax.dynamic_slice_in_dim(attended_all, start, own_rows, 0)
    result = (
        latents.astype(jnp.float32) + jnp.dot(attended, w_out, preferred_element_type=jnp.float32)
    ).astype(jnp.bfloat16)
    grad_all = lax.all_gather(grad_attended, "pts", axis=0, tiled=True)
    delta_all = jnp.sum(
        (grad_all.astype(jnp.float32) * attended_all.astype(jnp.float32)).reshape(
            query_count, HEADS, head_dim
        ),
        axis=2,
    )
    lse_all = row_max.T + jnp.log(total_all)

    def backward_head(operands):
        query_head, key_head, value_head, grad_head, lse_head, delta_head = operands
        probability = jnp.exp(masked_scores(query_head, key_head, live_mask) - lse_head[:, None])
        grad_value = jnp.dot(
            probability.astype(jnp.bfloat16).T, grad_head, preferred_element_type=jnp.float32
        )
        grad_weights = jnp.dot(grad_head, value_head.T, preferred_element_type=jnp.float32)
        grad_scores = (probability * (grad_weights - delta_head[:, None])).astype(jnp.bfloat16)
        grad_query = jnp.dot(grad_scores, key_head, preferred_element_type=jnp.float32) * 0.125
        grad_key = jnp.dot(grad_scores.T, query_head, preferred_element_type=jnp.float32) * 0.125
        return (grad_query, grad_key, grad_value)

    grad_query, grad_key, grad_value = lax.map(
        backward_head,
        (query_heads, key_heads, value_heads, split_heads(grad_all), lse_all.T, delta_all.T),
    )
    grad_query_own = lax.psum_scatter(
        join_heads(grad_query), "pts", scatter_dimension=0, tiled=True
    )
    d_latents = (
        d_out.astype(jnp.float32)
        + jnp.dot(
            grad_query_own.astype(jnp.bfloat16), w_query.T, preferred_element_type=jnp.float32
        )
    ).astype(jnp.bfloat16)
    d_points = (
        jnp.dot(
            join_heads(grad_key).astype(jnp.bfloat16), w_key.T, preferred_element_type=jnp.float32
        )
        + jnp.dot(
            join_heads(grad_value).astype(jnp.bfloat16),
            w_value.T,
            preferred_element_type=jnp.float32,
        )
    ).astype(jnp.bfloat16)
    return (result, d_latents, d_points)


def solution(mesh):
    in_specs = (
        P(("groups", "pts"), None),
        P(("groups", "pts"), None),
        P(("groups", "pts")),
        P(),
        P(),
        P(),
        P(),
        P(("groups", "pts"), None),
    )
    out_specs = (P(("groups", "pts"), None), P(("groups", "pts"), None), P(("groups", "pts"), None))
    return jax.shard_map(body, mesh=mesh, in_specs=in_specs, out_specs=out_specs, check_vma=False)
```

profile of v0, /device:TPU:0, one launch (start us, length us, event | category | flops | bytes accessed | tf_op | source)
XLA Modules:
  0.0 493.8 jit_solution(4530850203376139020)
XLA Ops:
  7.3 2.4 convolution_convert_fusion.3
  9.8 2.0 convolution_convert_fusion.2
  17.7 35.6 %all-gather.3.cloned.1.call-done = bf16[1024,768]{1,0:T(8,128)(2,1)} async-done(((bf16[64,768]{1,0:T(8,128)(2,1)}), bf16[1024,768]{1,0:T(8,128)(2,1)}) %all-gather.3.cloned.1.call-update) | async-done | bytes 1572880 | tf_op jit(solution)/shard_map/all_gather | solution.py:22
  55.0 2.7 copy.38
  57.8 25.9 %while.39 = (s32[]{:T(128)}, f32[12,1024]{1,0:T(8,128)S(1)}, bf16[12,1024,64]{2,1,0:T(8,128)(2,1)}, bf16[12,384,64]{2,1,0:T(8,128)(2,1)}, s32[]{:T(128)}, /*index=5*/s32[]{:T(128)}, s32[]{:T(128)}) while((s32[]{:T(128)}, f32[12,1024]{1,0:T(8,128)S(1)}, bf16[12,1024,64]{2,1,0:T(8,128)(2,1)}, bf16[12,384,64]{2,1,0:T(8,128)(2,1)}, ...), condition=%wide.region_2.3_spmd.clone, body=%wide.region_0.2_spmd.clone.sunk | while | flops 51510656 | bytes 374621 | solution.py:39
  83.6 59.7 %pmax.7 = f32[12,1024]{1,0:T(8,128)S(1)} all-reduce(f32[12,1024]{1,0:T(8,128)S(1)} %get-tuple-element.132), channel_id=1, replica_groups=mesh['groups'=2,'pts'=16] {'pts'}, use_global_device_ids=true, to_apply=%region_3.4 | all-reduce | flops 12288 | bytes 98304 | tf_op jit(solution)/shard_map/pmax | solution.py:39
  143.3 2.1 broadcast.28.clone
  145.4 50.3 %while.40 = (s32[]{:T(128)}, f32[12,1024]{1,0:T(8,128)S(1)}, f32[12,1024,64]{1,2,0:T(8,128)}, bf16[12,1024,64]{2,1,0:T(8,128)(2,1)}, bf16[12,384,64]{2,1,0:T(8,1...) while((s32[]{:T(128)}, f32[12,1024]{1,0:T(8,128)S(1)}, ...), condition=%wide.region_6.7_spmd.clone, body=%wide.region_4.6_spmd.clone.sunk | while | flops 102628736 | bytes 2321273 | solution.py:49
  195.7 3.6 copy.41
  199.4 58.6 %psum.15 = f32[1024,12]{0,1:T(8,128)S(1)} all-reduce(f32[1024,12]{0,1:T(8,128)S(1)} %bitcast.173), channel_id=1, replica_groups=mesh['groups'=2,'pts'=16] {'pts'}, use_global_device_ids=true, to_apply=%region_8.9 | all-reduce | flops 12288 | bytes 98304 | tf_op jit(solution)/shard_map/psum | solution.py:54
  258.0 2.0 broadcast_in_dim.58
  260.0 3.5 copy.42
  263.6 2.7 copy.43
  266.3 34.2 %all-reduce.2.cloned.1.call-done = f32[1024,768]{1,0:T(8,128)} async-done(((f32[1024,768]{1,0:T(8,128)}), f32[1024,768]{1,0:T(8,128)}) %all-reduce.2.cloned.1.call-update) | async-done | bytes 3145744 | tf_op jit(solution)/shard_map/psum | solution.py:54
  300.5 5.6 %convert_multiply_fusion = (f32[1024,768]{1,0:T(8,128)}, bf16[1024,768]{1,0:T(8,128)(2,1)}) fusion(bf16[1024,768]{1,0:T(8,128)(2,1)S(1)} %copy-done.1, f32[1024,768]{1,0:T(8,128)} %all-reduce.2.cloned.1.call-done, f32[1024,768]{1,0:T(8,128)} %copy.42), kind=kLoop, calls=%fused_computation.57 | loop fusion | flops 3932160 | bytes 12582912 | tf_op jit(solution)/shard_map/mul | solution.py:62
  306.1 3.6 copy.44
  309.7 2.3 reduce_sum.18
  311.9 2.1 broadcast.28
  314.0 102.0 %while.41 = (s32[]{:T(128)}, f32[12,1024,64]{1,2,0:T(8,128)}, bf16[12,384,64]{1,2,0:T(8,128)(2,1)}, bf16[12,384,64]{1,2,0:T(8,128)(2,1)S(1)}, bf16[12,1024,64]{2...) while((s32[]{:T(128)}, f32[12,1024,64]{1,2,0:T(8,128)}, ...), condition=%wide.region_11.12_spmd.clone, body=%wide.region_10.11_spmd.clone.sunk | while | flops 254501248 | bytes 8648581 | solution.py:81
  360.0 2.0 fusion.108
  368.5 2.0 fusion.108
  385.5 2.0 fusion.108
  416.0 3.5 copy.49
  426.1 58.9 %reduce-scatter.4.cloned.1.call-done = f32[64,768]{1,0:T(8,128)} async-done(((f32[1024,768]{1,0:T(8,128)}), f32[64,768]{1,0:T(8,128)}) %reduce-scatter.4.cloned.1.call-update) | async-done | bytes 196624
  (223 shorter events, 187.4 us)
Async XLA Ops:
  7.2 4.7 copy-start
  7.2 2.6 copy-start.3
  7.2 4.7 copy-start.9
  7.2 46.1 %all-gather.3.cloned.1.call-start = ((), (), s32[]{:S(2)}) async-start(), calls=%async_computation.1 | async-start | bytes 1671168 | tf_op jit(solution)/shard_map/all_gather | solution.py:22
  9.7 253.8 %all-gather.5.cloned.1.call-start = ((), (), s32[]{:S(2)}) async-start(), calls=%async_computation.3 | async-start | bytes 1671168 | tf_op jit(solution)/shard_map/all_gather | solution.py:60
  11.8 288.6 %all-reduce.2.cloned.1.call-start = ((), (), s32[]{:S(2)}) async-start(), calls=%async_computation.2 | async-start | bytes 6291456 | tf_op jit(solution)/shard_map/psum | solution.py:54
  12.6 1.8 copy-start.5
  199.3 285.7 %reduce-scatter.4.cloned.1.call-start = ((), (), s32[]{:S(2)}) async-start(), calls=%async_computation.4 | async-start | bytes 3342336
  263.6 36.9 %copy-start.1 = (bf16[1024,768]{1,0:T(8,128)(2,1)S(1)}, bf16[1024,768]{1,0:T(8,128)(2,1)}, u32[]{:S(2)}) copy-start(bf16[1024,768]{1,0:T(8,128)(2,1)} %all-gather.5.cloned.1.call-done) | copy-start | bytes 4718596
  419.6 1.3 copy-start.4
  419.6 1.3 copy-start.8
  422.7 1.8 copy-start.6
  424.6 61.6 %copy-start.2 = (bf16[768,768]{1,0:T(8,128)(2,1)S(1)}, bf16[768,768]{1,0:T(8,128)(2,1)}, u32[]{:S(2)}) copy-start(bf16[768,768]{1,0:T(8,128)(2,1)} %param.17) | copy-start | bytes 3538948
  424.6 61.6 %copy-start.7 = (bf16[64,768]{1,0:T(8,128)(2,1)S(1)}, bf16[64,768]{1,0:T(8,128)(2,1)}, u32[]{:S(2)}) copy-start(bf16[64,768]{1,0:T(8,128)(2,1)} %param.21) | copy-start | bytes 294916
Sparse Core Ops, SparseCore 0:
  10.9 42.3 all-gather.2
  56.1 38.5 all-gather.4
  199.4 101.0 all-reduce.1
  419.7 65.2 reduce-scatter.3
where the time goes:
time: 497 us; the launch traced here: 494 us
  matrix products  164 us (33%)
  waiting for transfers between devices  129 us (26%)
  blocking collectives  118 us (24%)
  local copies, waits for them, and re-layouts  36.3 us (7%)
  other arithmetic  31.3 us (6%)
  between operations  14 us (3%)
    pmax x1, blocking collectives, body(): row_max = lax.pmax(lax.map(local_max, (query_heads, key_heads)), 'pts')  59.7 us
    unnamed x5, waiting for transfers between devices  59 us
    psum x1, blocking collectives, body(): numer_all, total_all = lax.psum((numerator, total_cols), 'pts')  58.6 us
    dot_general x36, matrix products, masked_scores(): jnp.dot(query_head, key_head.T, preferred_element_type=jnp.float32) * 0.125  51.5 us
    all_gather x1, waiting for transfers between devices, body(): query_all = lax.all_gather(query_own, 'pts', axis=0, tiled=True)  35.6 us
    psum x1, waiting for transfers between devices, body(): numer_all, total_all = lax.psum((numerator, total_cols), 'pts')  34.2 us
    dot_general x12, matrix products, backward_head(): jnp.dot(grad_scores, key_head, preferred_element_type=jnp.float32) * 0.125  23.7 us
    lt x36, other arithmetic, body(): live_mask = jnp.arange(slots, dtype=jnp.int32) < counts[0]  23.4 us
  transfers between devices with their start and end apart: 4, of which 3 were waited for; matrix products, arithmetic and copies ran while one was open for 22% of the time, Pallas kernels for 0%

commit v1 on v0

--- a/solution.py
+++ b/solution.py
@@ -4,6 +4,28 @@
 from jax.sharding import PartitionSpec as P
 
 HEADS = 12
+
+
+def signs_find(vals, ndim_at):
+    response = list(vals.shape[1:])
+    response[ndim_at] *= vals.shape[0]
+    z_new = jnp.moveaxis(vals, 0, ndim_at).reshape(response)
+    return z_new
+
+
+def answer_ends(incoming_x, mesh_ax):
+    passed = lax.psum(1, axis_name=mesh_ax)
+    y = lax.axis_index(mesh_ax)
+    shaped, row_out = (passed, y)
+    a_next, seen_now = (incoming_x[None], 1)
+    while seen_now < shaped:
+        state_next = tuple(((dev_j, dev_j ^ seen_now) for dev_j in range(shaped)))
+        then = lax.ppermute(a_next, axis_name=mesh_ax, perm=state_next)
+        tile_out = row_out & seen_now == 0
+        out_arr = jnp.where(tile_out, a_next, then)
+        a_next = jnp.concatenate([out_arr, jnp.where(tile_out, then, a_next)])
+        seen_now *= 2
+    return a_next
 
 
 def masked_scores(query_head, key_head, live_mask):
@@ -19,7 +41,7 @@
     value_rows = jnp.dot(points, w_value, preferred_element_type=jnp.float32).astype(jnp.bfloat16)
     live_mask = jnp.arange(slots, dtype=jnp.int32) < counts[0]
     query_own = jnp.dot(latents, w_query, preferred_element_type=jnp.float32).astype(jnp.bfloat16)
-    query_all = lax.all_gather(query_own, "pts", axis=0, tiled=True)
+    query_all = signs_find(answer_ends(query_own, "pts"), 0)
     query_count = query_all.shape[0]
 
     def split_heads(matrix):

time: 497 us -> 522 us (1.050)
  local copies, waits for them, and re-layouts: 36.3 us -> 45 us
  starting transfers between devices: 0.16 us -> 8.02 us
    ppermute x0 -> x4, waiting for transfers between devices: none -> 40.6 us  [answer_ends(): then = lax.ppermute(a_next, axis_name=mesh_ax, perm=state_next)]
    all_gather x1 -> x0, waiting for transfers between devices: 35.6 us -> none  [body(): query_all = lax.all_gather(query_own, 'pts', axis=0, tiled=True)]
    ppermute x0 -> x4, starting transfers between devices: none -> 7.9 us  [answer_ends(): then = lax.ppermute(a_next, axis_name=mesh_ax, perm=state_next)]
    unnamed x5 -> x4, waiting for transfers between devices: 59 us -> 59 us
    unnamed x25 -> x23, local copies, waits for them, and re-layouts: 11.5 us -> 11.5 us
  transfers between devices with their start and end apart: 4 -> 7, of which waited for: 3 -> 6; matrix products, arithmetic and copies ran while one was open for 22% -> 23% of each run, Pallas kernels for 0% -> 0%
where the time goes in v1:
time: 522 us; the launch traced here: 519 us
  matrix products  164 us (31%)
  waiting for transfers between devices  134 us (26%)
  blocking collectives  120 us (23%)
  local copies, waits for them, and re-layouts  45 us (9%)
  other arithmetic  33 us (6%)
  between operations  14 us (3%)
  starting transfers between devices  8.02 us (2%)
    pmax x1, blocking collectives, body(): row_max = lax.pmax(lax.map(local_max, (query_heads, key_heads)), 'pts')  61.1 us
    unnamed x4, waiting for transfers between devices  59 us
    psum x1, blocking collectives, body(): numer_all, total_all = lax.psum((numerator, total_cols), 'pts')  58.7 us
    dot_general x36, matrix products, masked_scores(): jnp.dot(query_head, key_head.T, preferred_element_type=jnp.float32) * 0.125  51.6 us
    ppermute x4, waiting for transfers between devices, answer_ends(): then = lax.ppermute(a_next, axis_name=mesh_ax, perm=state_next)  40.6 us
    psum x1, waiting for transfers between devices, body(): numer_all, total_all = lax.psum((numerator, total_cols), 'pts')  34 us
    dot_general x12, matrix products, backward_head(): jnp.dot(grad_scores, key_head, preferred_element_type=jnp.float32) * 0.125  23.7 us
    lt x36, other arithmetic, body(): live_mask = jnp.arange(slots, dtype=jnp.int32) < counts[0]  23.4 us
  transfers between devices with their start and end apart: 7, of which 6 were waited for; matrix products, arithmetic and copies ran while one was open for 23% of the time, Pallas kernels for 0%

profile of v1, /device:TPU:0, one launch (start us, length us, event | category | flops | bytes accessed | tf_op | source)
XLA Modules:
  0.0 519.0 jit_solution(13181352839999559824)
XLA Ops:
  10.5 2.9 collective-permute-start.1
  13.4 5.2 %collective-permute-done.1 = bf16[2,64,768]{2,1,0:T(8,128)(2,1)S(1)} collective-permute-done((bf16[2,64,768]{2,1,0:T(8,128)(2,1)S(1)}, bf16[2,64,768]{2,1,0:T(8,128)(2,1)S(1)}, u32[]{:S(2)}, u32[]{:S(2)}) %collective-permute-start.1) | collective-permute-done | bytes 196640 | tf_op jit(solution)/shard_map/ppermute | solution.py:23
  20.6 8.8 %collective-permute-done.2 = bf16[4,64,768]{2,1,0:T(8,128)(2,1)S(1)} collective-permute-done((bf16[4,64,768]{2,1,0:T(8,128)(2,1)S(1)}, bf16[4,64,768]{2,1,0:T(8,128)(2,1)S(1)}, u32[]{:S(2)}, u32[]{:S(2)}) %collective-permute-start.2) | collective-permute-done | bytes 393248 | tf_op jit(solution)/shard_map/ppermute | solution.py:23
  29.6 2.6 collective-permute-start.3
  37.6 2.9 convolution_convert_fusion
  43.3 25.6 %collective-permute-done.3 = bf16[8,64,768]{2,1,0:T(8,128)(2,1)} collective-permute-done((bf16[8,64,768]{2,1,0:T(8,128)(2,1)S(1)}, bf16[8,64,768]{2,1,0:T(8,128)(2,1)}, u32[]{:S(2)}, u32[]{:S(2)}) %collective-permute-start.3) | collective-permute-done | bytes 786464 | tf_op jit(solution)/shard_map/ppermute | solution.py:23
  70.3 3.8 copy.33
  74.2 4.5 reshape_reshape.3
  78.6 2.7 copy.38
  81.4 25.9 %while.39 = (s32[]{:T(128)}, f32[12,1024]{1,0:T(8,128)S(1)}, bf16[12,1024,64]{2,1,0:T(8,128)(2,1)}, bf16[12,384,64]{2,1,0:T(8,128)(2,1)}, s32[]{:T(128)}, /*index=5*/s32[]{:T(128)}, s32[]{:T(128)}) while((s32[]{:T(128)}, f32[12,1024]{1,0:T(8,128)S(1)}, bf16[12,1024,64]{2,1,0:T(8,128)(2,1)}, bf16[12,384,64]{2,1,0:T(8,128)(2,1)}, ...), condition=%wide.region_2.3_spmd.clone, body=%wide.region_0.2_spmd.clone.sunk | while | flops 51510656 | bytes 374621 | solution.py:61
  107.3 61.1 %pmax.7 = f32[12,1024]{1,0:T(8,128)S(1)} all-reduce(f32[12,1024]{1,0:T(8,128)S(1)} %get-tuple-element.132), channel_id=1, replica_groups=mesh['groups'=2,'pts'=16] {'pts'}, use_global_device_ids=true, to_apply=%region_3.4 | all-reduce | flops 12288 | bytes 98304 | tf_op jit(solution)/shard_map/pmax | solution.py:61
  168.4 2.1 broadcast.28.clone
  170.5 50.4 %while.40 = (s32[]{:T(128)}, f32[12,1024]{1,0:T(8,128)S(1)}, f32[12,1024,64]{1,2,0:T(8,128)}, bf16[12,1024,64]{2,1,0:T(8,128)(2,1)}, bf16[12,384,64]{2,1,0:T(8,1...) while((s32[]{:T(128)}, f32[12,1024]{1,0:T(8,128)S(1)}, ...), condition=%wide.region_6.7_spmd.clone, body=%wide.region_4.6_spmd.clone.sunk | while | flops 102628736 | bytes 2321273 | solution.py:71
  220.9 3.6 copy.41
  224.6 58.7 %psum.15 = f32[1024,12]{0,1:T(8,128)S(1)} all-reduce(f32[1024,12]{0,1:T(8,128)S(1)} %bitcast.175), channel_id=1, replica_groups=mesh['groups'=2,'pts'=16] {'pts'}, use_global_device_ids=true, to_apply=%region_8.9 | all-reduce | flops 12288 | bytes 98304 | tf_op jit(solution)/shard_map/psum | solution.py:76
  285.3 3.5 copy.42
  288.9 2.7 copy.43
  291.6 34.0 %all-reduce.2.cloned.1.call-done = f32[1024,768]{1,0:T(8,128)} async-done(((f32[1024,768]{1,0:T(8,128)}), f32[1024,768]{1,0:T(8,128)}) %all-reduce.2.cloned.1.call-update) | async-done | bytes 3145744 | tf_op jit(solution)/shard_map/psum | solution.py:76
  325.6 5.6 %convert_multiply_fusion = (f32[1024,768]{1,0:T(8,128)}, bf16[1024,768]{1,0:T(8,128)(2,1)}) fusion(bf16[1024,768]{1,0:T(8,128)(2,1)S(1)} %copy-done.1, f32[1024,768]{1,0:T(8,128)} %all-reduce.2.cloned.1.call-done, f32[1024,768]{1,0:T(8,128)} %copy.42), kind=kLoop, calls=%fused_computation.57 | loop fusion | flops 3932160 | bytes 12582912 | tf_op jit(solution)/shard_map/mul | solution.py:84
  331.3 3.6 copy.44
  334.8 2.3 reduce_sum.18
  339.2 102.0 %while.41 = (s32[]{:T(128)}, f32[12,1024,64]{1,2,0:T(8,128)}, bf16[12,384,64]{1,2,0:T(8,128)(2,1)}, bf16[12,384,64]{1,2,0:T(8,128)(2,1)S(1)}, bf16[12,1024,64]{2...) while((s32[]{:T(128)}, f32[12,1024,64]{1,2,0:T(8,128)}, ...), condition=%wide.region_11.12_spmd.clone, body=%wide.region_10.11_spmd.clone.sunk | while | flops 254501248 | bytes 8648581 | solution.py:103
  441.2 3.5 copy.49
  451.3 59.0 %reduce-scatter.4.cloned.1.call-done = f32[64,768]{1,0:T(8,128)} async-done(((f32[1024,768]{1,0:T(8,128)}), f32[64,768]{1,0:T(8,128)}) %reduce-scatter.4.cloned.1.call-update) | async-done | bytes 196624
  (235 shorter events, 204.9 us)
Async XLA Ops:
  7.2 26.2 %copy-start = (bf16[768,768]{1,0:T(8,128)(2,1)S(1)}, bf16[768,768]{1,0:T(8,128)(2,1)}, u32[]{:S(2)}) copy-start(bf16[768,768]{1,0:T(8,128)(2,1)} %param.18) | copy-start | bytes 3538948
  7.2 281.7 %all-gather.2.cloned.1.call-start = ((), (), s32[]{:S(2)}) async-start(), calls=%async_computation.2 | async-start | bytes 1671168 | tf_op jit(solution)/shard_map/all_gather | solution.py:82
  9.0 1.5 collective-permute-start
  10.5 8.1 %collective-permute-start.1 = (bf16[2,64,768]{2,1,0:T(8,128)(2,1)S(1)}, bf16[2,64,768]{2,1,0:T(8,128)(2,1)S(1)}, u32[]{:S(2)}, u32[]{:S(2)}) collective-permute-start(bf16[2,64,768]{2,1,0:T(8,128)(2,1)S(1)} %pad_maximum_fusion.3), channel_id=1, source_target_pairs={{0,2},{1,3},{2,0},{3,1},{4,6},{5,7},{6,4},{7,5},{8,10},{9,11},{10,... | collective-permute-start | bytes 589832 | tf_op jit(solution)/shard_map/ppermute | solution.py:23
  18.7 10.7 %collective-permute-start.2 = (bf16[4,64,768]{2,1,0:T(8,128)(2,1)S(1)}, bf16[4,64,768]{2,1,0:T(8,128)(2,1)S(1)}, u32[]{:S(2)}, u32[]{:S(2)}) collective-permute-start(bf16[4,64,768]{2,1,0:T(8,128)(2,1)S(1)} %pad_maximum_fusion.2), channel_id=1, source_target_pairs={{0,4},{1,5},{2,6},{3,7},{4,0},{5,1},{6,2},{7,3},{8,12},{9,13},{10,... | collective-permute-start | bytes 1179656 | tf_op jit(solution)/shard_map/ppermute | solution.py:23
  20.6 11.6 %copy-start.3 = (bf16[768,768]{1,0:T(8,128)(2,1)S(1)}, bf16[768,768]{1,0:T(8,128)(2,1)}, u32[]{:S(2)}) copy-start(bf16[768,768]{1,0:T(8,128)(2,1)} %param.20) | copy-start | bytes 3538948
  20.6 11.6 %copy-start.6 = (bf16[64,768]{1,0:T(8,128)(2,1)S(1)}, bf16[64,768]{1,0:T(8,128)(2,1)}, u32[]{:S(2)}) copy-start(bf16[64,768]{1,0:T(8,128)(2,1)} %param.21) | copy-start | bytes 294916
  29.5 3.9 copy-start.8
  29.6 39.4 %collective-permute-start.3 = (bf16[8,64,768]{2,1,0:T(8,128)(2,1)S(1)}, bf16[8,64,768]{2,1,0:T(8,128)(2,1)}, u32[]{:S(2)}, u32[]{:S(2)}) collective-permute-start(bf16[8,64,768]{2,1,0:T(8,128)(2,1)S(1)} %pad_maximum_fusion.1), channel_id=1, source_target_pairs={{0,8},{1,9},{2,10},{3,11},{4,12},{5,13},{6,14},{7,15},{8,0},{9,1},... | collective-permute-start | bytes 2359304 | tf_op jit(solution)/shard_map/ppermute | solution.py:23
  33.3 292.3 %all-reduce.2.cloned.1.call-start = ((), (), s32[]{:S(2)}) async-start(), calls=%async_computation.1 | async-start | bytes 6291456 | tf_op jit(solution)/shard_map/psum | solution.py:76
  224.5 285.8 %reduce-scatter.4.cloned.1.call-start = ((), (), s32[]{:S(2)}) async-start(), calls=%async_computation.3 | async-start | bytes 3342336
  288.9 36.7 %copy-start.1 = (bf16[1024,768]{1,0:T(8,128)(2,1)S(1)}, bf16[1024,768]{1,0:T(8,128)(2,1)}, u32[]{:S(2)}) copy-start(bf16[1024,768]{1,0:T(8,128)(2,1)} %all-gather.2.cloned.1.call-done) | copy-start | bytes 4718596
  444.8 1.3 copy-start.4
  444.8 1.3 copy-start.7
  447.9 1.8 copy-start.5
  449.7 61.6 %copy-start.2 = (bf16[768,768]{1,0:T(8,128)(2,1)S(1)}, bf16[768,768]{1,0:T(8,128)(2,1)}, u32[]{:S(2)}) copy-start(bf16[768,768]{1,0:T(8,128)(2,1)} %param.17) | copy-start | bytes 3538948
Sparse Core Ops, SparseCore 0:
  33.4 57.2 all-gather.1
  224.6 100.9 all-reduce.1
  444.9 65.3 reduce-scatter.3
